TPU v7x, 32 devices: a whole 2x2x4 slice. The times are simulated.
32 devices in a mesh: head: 4 (over y, x), blk: 8 (over z, core).
Axes of the slice: x: 2, y: 2, z: 4, core: 2. Of those that a mesh axis runs over, the one named last changes fastest.
Arguments:
- queries: bfloat16 [4096, 2048], P(('blk', 'head')), may hold values from -8 to 8
- keys: bfloat16 [4096, 2048], P(('blk', 'head')), may hold values from -8 to 8
- values: bfloat16 [4096, 2048], P(('blk', 'head')), may hold values from -6 to 6
- grad_out: bfloat16 [4096, 2048], P(('blk', 'head')), may hold values from -6 to 6
- stride_owner: int32 [32, 3], replicated, may hold values from 0 to 7, all different within a row; in each aligned block of 4 rows (0 to 3, 4 to 7, ...) at most 2 rows name the same one
Outputs:
- attended: bfloat16 [4096, 2048], P('blk', 'head')
- grad_queries: bfloat16 [4096, 2048], P('blk', 'head')
- grad_keys: bfloat16 [4096, 2048], P('blk', 'head')
- grad_values: bfloat16 [4096, 2048], P('blk', 'head')
Inputs may be any that keep to these rules, and one draw needn't show every extreme that they name: `stride_owner`: each row names 3 different runs. Within each aligned block of 4 rows no run is named by more than 2 rows, a bound that some block reaches.
All inputs are finite; a program needn't handle non-finite values.
Results may differ from a plain program's by a relative error of at most 0.02.
Values may be sent and summed in bfloat16 or wider, within the bound.
A program may use at most 128 MiB of HBM per device.

v0:
```python
import math
from functools import partial

import jax
import jax.numpy as jnp
from jax import lax
from jax.experimental import pallas as pl
from jax.experimental.pallas import tpu as pltpu
from jax.sharding import PartitionSpec as P

HEAD_DIM = 128
BLOCK = 128
PICKS = 3
MESH = pl.DeviceIdType.MESH


def with_halo(block, sides, width):
    for axis, dim in sides:
        count = lax.axis_size(axis)
        forward = [(i, i + 1) for i in range(count - 1)]
        forward.append((count - 1, 0))
        backward = [(target, source) for source, target in forward]
        low = lax.ppermute(
            lax.slice_in_dim(block, block.shape[dim] - width, None, axis=dim), axis, forward
        )
        high = lax.ppermute(lax.slice_in_dim(block, 0, width, axis=dim), axis, backward)
        block = jnp.concatenate([low, block, high], axis=dim)
    return block


def from_root(block, axis, holder):
    block = jnp.where(lax.axis_index(axis) == holder, block, jnp.zeros_like(block))
    return lax.psum(block, axis)


def slot_tables(stride_owner, n_blk, blocks, capacity, device):
    owner_table = stride_owner.reshape(n_blk, blocks, PICKS)
    owner_ids = jnp.arange(n_blk, dtype=jnp.int32)
    naming = jnp.any(owner_table[:, :, :, None] == owner_ids[None, None, None, :], axis=2)
    counts = naming.astype(jnp.int32)
    ranking = jnp.cumsum(counts, axis=1) - counts
    naming_here = lax.dynamic_index_in_dim(naming, device, 2, keepdims=False)
    ranking_here = lax.dynamic_index_in_dim(ranking, device, 2, keepdims=False)
    slot_ids = jnp.arange(capacity, dtype=jnp.int32)
    matched = naming_here[:, None, :] & (ranking_here[:, None, :] == slot_ids[None, :, None])
    offsets = jnp.sum(
        matched.astype(jnp.int32) * jnp.arange(blocks, dtype=jnp.int32)[None, None, :], axis=2
    )
    own_rows = lax.dynamic_index_in_dim(owner_table, device, 0, keepdims=False)
    own_ranks = lax.dynamic_index_in_dim(ranking, device, 0, keepdims=False)
    picked = jnp.take_along_axis(own_ranks, own_rows, axis=1)
    flat_slot = own_rows * capacity + picked
    return (offsets.reshape(-1), flat_slot, matched.reshape(n_blk * capacity, blocks))


def fetch_keys(stacked, offsets, flat_slot, capacity):
    seq_rows = stacked.shape[1]
    width = stacked.shape[2]
    blocks = seq_rows // BLOCK
    n_blk = lax.axis_size("blk")
    extended = with_halo(stacked, (("blk", 1),), BLOCK)
    extended = extended.reshape(2, blocks + 2, BLOCK, width)
    block_view = stacked.reshape(2, blocks, BLOCK, width)
    leading = from_root(block_view[:, 0:2], "blk", 0)
    outgoing = jnp.take(block_view, offsets, axis=1).reshape(2, n_blk, capacity, BLOCK, width)
    incoming = lax.all_to_all(outgoing, "blk", split_axis=1, concat_axis=1, tiled=True)
    incoming = incoming.reshape(2, n_blk * capacity, BLOCK, width)
    pooled = jnp.concatenate([extended, incoming, leading], axis=1)
    rows_here = jnp.arange(blocks, dtype=jnp.int32)[:, None]
    nearby_index = rows_here + jnp.arange(3, dtype=jnp.int32)[None, :]
    distant_index = blocks + 2 + flat_slot
    leading_index = (
        jnp.zeros((blocks, 2), jnp.int32)
        + (blocks + 2 + n_blk * capacity)
        + jnp.arange(2, dtype=jnp.int32)[None, :]
    )
    table = jnp.concatenate([nearby_index, distant_index, leading_index], axis=1)
    return jnp.take(pooled, table.reshape(-1), axis=1)


def score_block(query_part, key_part, factor):
    return (
        jnp.einsum("gqhd,gjkhd->ghqjk", query_part, key_part, preferred_element_type=jnp.float32)
        * factor
    )


def log_normal(scores):
    row_max = jnp.max(scores, axis=(3, 4), keepdims=True)
    return row_max + jnp.log(jnp.sum(jnp.exp(scores - row_max), axis=(3, 4), keepdims=True))


def output_of(rounded, value_part):
    return jnp.einsum(
        "ghqjk,gjkhd->gqhd", rounded, value_part, preferred_element_type=jnp.float32
    ).astype(jnp.bfloat16)


def split_terms(coeffs, source):
    group_size = source.shape[0]
    near = jnp.einsum(
        "ghqjk,gqhd->gjkhd", coeffs[:, :, :, 0:3], source, preferred_element_type=jnp.float32
    )
    far = jnp.einsum(
        "ghqjk,gqhd->gjkhd", coeffs[:, :, :, 3:6], source, preferred_element_type=jnp.float32
    ).astype(jnp.bfloat16)
    lead = jnp.einsum(
        "ghqjk,gqhd->jkhd", coeffs[:, :, :, 6:8], source, preferred_element_type=jnp.float32
    )
    near = near.reshape(group_size, 3, near.shape[2], near.shape[3] * near.shape[4])
    far = far.reshape(group_size, 3, far.shape[2], far.shape[3] * far.shape[4])
    lead = lead.reshape(2, lead.shape[1], lead.shape[2] * lead.shape[3])
    return (near, far, lead)


def backward_from(
    scores, log_total, rounded, attended, grad_part, query_part, key_part, value_part, factor
):
    grad_weights = jnp.einsum(
        "gqhd,gjkhd->ghqjk", grad_part, value_part, preferred_element_type=jnp.float32
    )
    delta = jnp.sum(grad_part.astype(jnp.float32) * attended.astype(jnp.float32), axis=3)
    delta = jnp.transpose(delta, (0, 2, 1))[:, :, :, None, None]
    grad_scores = (jnp.exp(scores - log_total) * (grad_weights - delta) * factor).astype(
        jnp.bfloat16
    )
    grad_query = jnp.einsum(
        "ghqjk,gjkhd->gqhd", grad_scores, key_part, preferred_element_type=jnp.float32
    ).astype(jnp.bfloat16)
    key_near, key_far, key_lead = split_terms(grad_scores, query_part)
    value_near, value_far, value_lead = split_terms(rounded, grad_part)
    return (grad_query, key_near, key_far, key_lead, value_near, value_far, value_lead)


def spread_near(near_terms, width):
    blank = jnp.zeros((1, BLOCK, width), jnp.float32)
    return (
        jnp.concatenate([near_terms[:, 0], blank, blank], axis=0)
        + jnp.concatenate([blank, near_terms[:, 1], blank], axis=0)
        + jnp.concatenate([blank, blank, near_terms[:, 2]], axis=0)
    )


def by_runs(queries, keys, values, grad_out, stride_owner):
    query_rows, key_rows, value_rows, grad_rows = (
        lax.all_to_all(queries, "head", split_axis=1, concat_axis=0, tiled=True),
        lax.all_to_all(keys, "head", split_axis=1, concat_axis=0, tiled=True),
        lax.all_to_all(values, "head", split_axis=1, concat_axis=0, tiled=True),
        lax.all_to_all(grad_out, "head", split_axis=1, concat_axis=0, tiled=True),
    )
    seq_rows, width = query_rows.shape
    heads_here = width // HEAD_DIM
    blocks = seq_rows // BLOCK
    n_blk = lax.axis_size("blk")
    capacity = max(2, (PICKS * blocks + n_blk - 1) // n_blk)
    device = lax.axis_index("blk")
    offsets, flat_slot, matched = slot_tables(stride_owner, n_blk, blocks, capacity, device)
    group_size = math.gcd(blocks, max(1, 512 // BLOCK))
    group_count = blocks // group_size
    factor = HEAD_DIM ** (-0.5)
    stacked = jnp.stack([key_rows, value_rows])
    query_view = query_rows.reshape(blocks, BLOCK, heads_here, HEAD_DIM)
    grad_view = grad_rows.reshape(blocks, BLOCK, heads_here, HEAD_DIM)
    key_sets = fetch_keys(stacked, offsets, flat_slot, capacity)
    key_sets = key_sets.reshape(2, blocks, 8, BLOCK, heads_here, HEAD_DIM)

    def pieces(group_id):
        start = group_id * group_size
        query_part = lax.dynamic_slice_in_dim(query_view, start, group_size, 0)
        grad_part = lax.dynamic_slice_in_dim(grad_view, start, group_size, 0)
        kv_part = lax.dynamic_slice_in_dim(key_sets, start, group_size, 1)
        return (query_part, grad_part, kv_part[0], kv_part[1])

    def joined_pass(group_id):
        query_part, grad_part, key_part, value_part = pieces(group_id)
        scores = score_block(query_part, key_part, factor)
        log_total = log_normal(scores)
        rounded = jnp.exp(scores - log_total).astype(jnp.bfloat16)
        attended = output_of(rounded, value_part)
        extra = backward_from(
            scores,
            log_total,
            rounded,
            attended,
            grad_part,
            query_part,
            key_part,
            value_part,
            factor,
        )
        return (attended,) + extra

    group_ids = jnp.arange(group_count, dtype=jnp.int32)
    results = lax.map(joined_pass, group_ids)
    attended = results[0]
    grad_query, key_near, key_far, key_lead, value_near, value_far, value_lead = results[1:]
    key_ext = spread_near(key_near.reshape(blocks, 3, BLOCK, width), width)
    value_ext = spread_near(value_near.reshape(blocks, 3, BLOCK, width), width)
    rim_terms = jnp.stack(
        [
            jnp.stack([key_ext[0], value_ext[0]]),
            jnp.stack([key_ext[blocks + 1], value_ext[blocks + 1]]),
        ]
    )
    beside = with_halo(rim_terms.astype(jnp.bfloat16), (("blk", 0),), 1).astype(rim_terms.dtype)
    key_owned = key_ext[1 : blocks + 1].at[0].add(beside[0, 0]).at[blocks - 1].add(beside[3, 0])
    value_owned = value_ext[1 : blocks + 1].at[0].add(beside[0, 1]).at[blocks - 1].add(beside[3, 1])
    slot_flat = flat_slot.reshape(-1)
    key_back = (
        jnp.zeros((n_blk * capacity, BLOCK, width), jnp.bfloat16)
        .at[slot_flat]
        .set(key_far.reshape(blocks * PICKS, BLOCK, width))
    )
    value_back = (
        jnp.zeros((n_blk * capacity, BLOCK, width), jnp.bfloat16)
        .at[slot_flat]
        .set(value_far.reshape(blocks * PICKS, BLOCK, width))
    )
    key_arrived, value_arrived = (
        lax.all_to_all(
            key_back.reshape(n_blk, capacity, BLOCK, width),
            "blk",
            split_axis=0,
            concat_axis=0,
            tiled=True,
        ),
        lax.all_to_all(
            value_back.reshape(n_blk, capacity, BLOCK, width),
            "blk",
            split_axis=0,
            concat_axis=0,
            tiled=True,
        ),
    )
    match_b = matched.astype(jnp.bfloat16)
    key_owned = key_owned + jnp.einsum(
        "sr,sbc->rbc",
        match_b,
        key_arrived.reshape(n_blk * capacity, BLOCK, width),
        preferred_element_type=jnp.float32,
    )
    value_owned = value_owned + jnp.einsum(
        "sr,sbc->rbc",
        match_b,
        value_arrived.reshape(n_blk * capacity, BLOCK, width),
        preferred_element_type=jnp.float32,
    )
    key_total, value_total = (
        lax.psum(jnp.sum(key_lead, axis=0).astype(jnp.bfloat16), "blk").astype(jnp.float32),
        lax.psum(jnp.sum(value_lead, axis=0).astype(jnp.bfloat16), "blk").astype(jnp.float32),
    )
    at_root = device == 0
    key_owned = key_owned.at[0:2].add(jnp.where(at_root, key_total, jnp.zeros_like(key_total)))
    value_owned = value_owned.at[0:2].add(
        jnp.where(at_root, value_total, jnp.zeros_like(value_total))
    )
    grad_keys = key_owned.astype(jnp.bfloat16).reshape(seq_rows, width)
    grad_values = value_owned.astype(jnp.bfloat16).reshape(seq_rows, width)
    return (
        attended.reshape(seq_rows, width),
        grad_query.reshape(seq_rows, width),
        grad_keys,
        grad_values,
    )


def exchange_barrier(peers):
    barrier = pltpu.get_barrier_semaphore()
    for peer in peers:
        pl.semaphore_signal(barrier, inc=1, device_id=peer, device_id_type=MESH)
    pl.semaphore_wait(barrier, len(peers))


def head_kernel(
    n_head,
    n_z,
    owner_ref,
    q_in,
    k_in,
    v_in,
    g_in,
    o_out,
    dq_out,
    dk_out,
    dv_out,
    q_all,
    k_all,
    v_all,
    g_all,
    k_sum,
    v_sum,
    k_far,
    v_far,
    o_stage,
    dq_stage,
    dk_stage,
    dv_stage,
    k_give,
    v_give,
    k_take,
    v_take,
    in_send,
    in_recv,
    pass_send,
    pass_recv,
    own_sem,
    out_send,
    out_recv,
    out_own,
    pair_send,
    pair_recv,
):
    head = lax.axis_index("head")
    blk = lax.axis_index("blk")
    z = blk // 2
    c = blk % 2
    runs = n_head
    total_blocks = 2 * n_z * runs
    factor = HEAD_DIM ** (-0.5)
    sibling = {"head": head, "blk": 2 * z + 1 - c}
    offsets = [(dz, dh) for dz in range(n_z) for dh in range(n_head)]
    far_first = [dz for dz in (2, 1, 3, 0) if dz < n_z] + list(range(4, n_z))
    near_first = [0] + [dz for dz in far_first if dz != 0][::-1]

    def columns(head_id):
        return pl.ds(pl.multiple_of(head_id * HEAD_DIM, HEAD_DIM), HEAD_DIM)

    def to_peer(dz, dh):
        return (z + dz) % n_z, (head + dh) % n_head

    def from_peer(dz, dh):
        return (z + n_z - dz) % n_z, (head + n_head - dh) % n_head

    peers = []
    for dz, dh in offsets:
        if (dz, dh) != (0, 0):
            z2, h2 = to_peer(dz, dh)
            peers.append({"head": h2, "blk": 2 * z2 + c})
    exchange_barrier(peers + [sibling])

    key_pairs = ((0, k_in, k_all), (1, v_in, v_all))
    row_pairs = ((2, q_in, q_all), (3, g_in, g_all))
    mine = blk * runs + head
    my_row = z * runs + head
    my_head = head * n_z + z

    def push(at, source, target, slot, dz, dh):
        z2, h2 = to_peer(dz, dh)
        return pltpu.make_async_remote_copy(
            src_ref=source.at[:, columns(h2 * n_z + z2)],
            dst_ref=target.at[slot],
            send_sem=in_send.at[at, z2 * n_head + h2],
            recv_sem=in_recv.at[at, my_row],
            device_id={"head": h2, "blk": 2 * z2 + c},
            device_id_type=MESH,
        )

    def arrival(at, source, target, slot, dz, dh):
        z1, h1 = from_peer(dz, dh)
        return pltpu.make_async_remote_copy(
            src_ref=source.at[:, columns(my_head)],
            dst_ref=target.at[slot],
            send_sem=in_send.at[at, z1 * n_head + h1],
            recv_sem=in_recv.at[at, z1 * n_head + h1],
            device_id=sibling,
            device_id_type=MESH,
        )

    sends = []
    own_copies = []
    for at, source, target in key_pairs:
        own_copies.append(
            pltpu.make_async_copy(
                source.at[:, columns(my_head)], target.at[mine], own_sem.at[at]
            )
        )
        own_copies[-1].start()
    for dz in far_first:
        for dh in range(n_head):
            if (dz, dh) == (0, 0):
                continue
            for at, source, target in key_pairs:
                copy = push(at, source, target, mine, dz, dh)
                copy.start()
                sends.append(copy)
    passes = []
    for at, source, target in key_pairs:
        copy = pltpu.make_async_remote_copy(
            src_ref=source.at[:, columns(my_head)],
            dst_ref=target.at[mine],
            send_sem=pass_send.at[at, my_row],
            recv_sem=pass_recv.at[at, my_row],
            device_id=sibling,
            device_id_type=MESH,
        )
        copy.start()
        passes.append(copy)
    for at, source, target in row_pairs:
        own_copies.append(
            pltpu.make_async_copy(
                source.at[:, columns(my_head)], target.at[my_row], own_sem.at[at]
            )
        )
        own_copies[-1].start()
    for dz in near_first:
        for dh in range(n_head):
            if (dz, dh) == (0, 0):
                continue
            for at, source, target in row_pairs:
                copy = push(at, source, target, my_row, dz, dh)
                copy.start()
                sends.append(copy)

    blank = jnp.zeros((BLOCK, HEAD_DIM), jnp.float32)

    def clear(n, carry):
        k_sum[n] = blank
        v_sum[n] = blank
        return carry

    lax.fori_loop(0, total_blocks, clear, 0)
    none = n_z * runs * PICKS
    k_far[none] = blank.astype(jnp.bfloat16)
    v_far[none] = blank.astype(jnp.bfloat16)

    for dz in [0] + [d for d in far_first if d != 0]:
        for dh in range(n_head):
            if (dz, dh) == (0, 0):
                continue
            z1, h1 = from_peer(dz, dh)
            block = (2 * z1 + c) * runs + h1
            for at, source, target in key_pairs:
                arrival(at, source, target, block, dz, dh).wait_recv()
                copy = pltpu.make_async_remote_copy(
                    src_ref=target.at[block],
                    dst_ref=target.at[block],
                    send_sem=pass_send.at[at, z1 * n_head + h1],
                    recv_sem=pass_recv.at[at, z1 * n_head + h1],
                    device_id=sibling,
                    device_id_type=MESH,
                )
                copy.start()
                passes.append(copy)
    for copy in own_copies:
        copy.wait()
    for row in range(n_z * n_head):
        z1, h1 = row // n_head, row % n_head
        block = (2 * z1 + 1 - c) * runs + h1
        for at, source, target in key_pairs:
            pltpu.make_async_remote_copy(
                src_ref=target.at[block],
                dst_ref=target.at[block],
                send_sem=pass_send.at[at, row],
                recv_sem=pass_recv.at[at, row],
                device_id=sibling,
                device_id_type=MESH,
            ).wait_recv()

    def contract(left, right, dims):
        return lax.dot_general(
            left, right, ((dims[:1], dims[1:]), ((), ())), preferred_element_type=jnp.float32
        )

    def query_step(z1, r):
        row = z1 * runs + r
        block = (2 * z1 + c) * runs + r
        low = (block + total_blocks - 1) % total_blocks
        high = (block + 1) % total_blocks
        picks = [owner_ref[block, j] * runs + r for j in range(PICKS)]
        named = [low, block, high] + picks + [0, 1]
        keys = jnp.concatenate([k_all[n] for n in named], axis=0)
        values = jnp.concatenate([v_all[n] for n in named], axis=0)
        query = q_all[row]
        grad = g_all[row]
        scores = contract(keys, query, (1, 1))
        top = jnp.max(scores, axis=0, keepdims=True)
        weights = jnp.exp((scores - top) * factor)
        weights = weights * (1.0 / jnp.sum(weights, axis=0, keepdims=True))
        rounded = weights.astype(jnp.bfloat16)
        grad_weights = contract(values, grad, (1, 1))
        delta = jnp.sum(weights * grad_weights, axis=0, keepdims=True)
        grad_scores = (weights * (grad_weights - delta) * factor).astype(jnp.bfloat16)
        o_stage[row] = contract(rounded, values, (0, 0)).astype(jnp.bfloat16)
        dq_stage[row] = contract(grad_scores, keys, (0, 0)).astype(jnp.bfloat16)
        key_terms = contract(grad_scores, query, (1, 0))
        value_terms = contract(rounded, grad, (1, 0))
        for j, n in ((0, low), (1, block), (2, high), (6, 0), (7, 1)):
            k_sum[n] += key_terms[j * BLOCK : (j + 1) * BLOCK]
            v_sum[n] += value_terms[j * BLOCK : (j + 1) * BLOCK]
        for j in range(PICKS):
            rows = slice((3 + j) * BLOCK, (4 + j) * BLOCK)
            k_far[row * PICKS + j] = key_terms[rows].astype(jnp.bfloat16)
            v_far[row * PICKS + j] = value_terms[rows].astype(jnp.bfloat16)

    def hand_out(pairs, dz):
        for at, stage, out in pairs:
            z2 = (z + n_z - dz) % n_z
            for r in range(runs):
                source = stage.at[z2 * runs + r]
                rows = pl.ds(r * BLOCK, BLOCK)
                if dz == 0:
                    copy = pltpu.make_async_copy(
                        source, out.at[rows, columns(z)], out_own.at[at, r]
                    )
                    copy.start()
                    own_outs.append(copy)
                else:
                    copy = pltpu.make_async_remote_copy(
                        src_ref=source,
                        dst_ref=out.at[rows, columns(z)],
                        send_sem=out_send.at[at, z2 * runs + r],
                        recv_sem=out_recv.at[at, z * runs + r],
                        device_id={"head": head, "blk": 2 * z2 + c},
                        device_id_type=MESH,
                    )
                    copy.start()
                    sends.append(copy)

    own_outs = []
    row_outs = ((0, o_stage, o_out), (1, dq_stage, dq_out))
    key_outs = ((2, dk_stage, dk_out), (3, dv_stage, dv_out))
    for dz in near_first:
        z1 = (z + n_z - dz) % n_z
        for dh in range(n_head):
            if (dz, dh) == (0, 0):
                continue
            h1 = (head + n_head - dh) % n_head
            for at, source, target in row_pairs:
                arrival(at, source, target, z1 * runs + h1, dz, dh).wait_recv()

        def step(r, carry, z1=z1):
            query_step(z1, r)
            return carry

        lax.fori_loop(0, runs, step, 0)
        hand_out(row_outs, dz)

    def total_of(sums, far, run, r):
        total = sums[run * runs + r]
        for z1 in range(n_z):
            block = (2 * z1 + c) * runs + r
            row = z1 * runs + r
            place = none
            for j in range(PICKS):
                place = jnp.where(owner_ref[block, j] == run, row * PICKS + j, place)
            total = total + far[place].astype(jnp.float32)
        return total

    def give_step(row, carry):
        run, r = 2 * (row // runs) + 1 - c, row % runs
        k_give[row] = total_of(k_sum, k_far, run, r).astype(jnp.bfloat16)
        v_give[row] = total_of(v_sum, v_far, run, r).astype(jnp.bfloat16)
        return carry

    lax.fori_loop(0, n_z * runs, give_step, 0)
    pair_copies = []
    for at, give, take in ((0, k_give, k_take), (1, v_give, v_take)):
        copy = pltpu.make_async_remote_copy(
            src_ref=give,
            dst_ref=take,
            send_sem=pair_send.at[at],
            recv_sem=pair_recv.at[at],
            device_id=sibling,
            device_id_type=MESH,
        )
        copy.start()
        pair_copies.append(copy)
    for copy in pair_copies:
        copy.wait_recv()
    for dz in far_first:
        z1 = (z + n_z - dz) % n_z

        def join_step(r, carry, z1=z1):
            row, run = z1 * runs + r, 2 * z1 + c
            for sums, far, take, stage in (
                (k_sum, k_far, k_take, dk_stage),
                (v_sum, v_far, v_take, dv_stage),
            ):
                total = total_of(sums, far, run, r) + take[row].astype(jnp.float32)
                stage[row] = total.astype(jnp.bfloat16)
            return carry

        lax.fori_loop(0, runs, join_step, 0)
        hand_out(key_outs, dz)

    for dz in range(1, n_z):
        z1 = (z + n_z - dz) % n_z
        for at, stage, out in row_outs + key_outs:
            for r in range(runs):
                pltpu.make_async_remote_copy(
                    src_ref=stage.at[z1 * runs + r],
                    dst_ref=out.at[pl.ds(r * BLOCK, BLOCK), columns(z1)],
                    send_sem=out_send.at[at, z1 * runs + r],
                    recv_sem=out_recv.at[at, z1 * runs + r],
                    device_id=sibling,
                    device_id_type=MESH,
                ).wait_recv()
    for copy in own_outs:
        copy.wait()
    for copy in sends + passes + pair_copies:
        copy.wait_send()


def by_heads(queries, keys, values, grad_out, stride_owner):
    n_head, n_blk = lax.axis_size("head"), lax.axis_size("blk")
    n_z = n_blk // 2
    rows = n_z * n_head
    seq_rows, width = BLOCK * n_head, n_z * HEAD_DIM
    tile = (BLOCK, HEAD_DIM)
    low, wide = jnp.bfloat16, jnp.float32
    dma = pltpu.SemaphoreType.DMA
    out = jax.ShapeDtypeStruct((seq_rows, width), low)
    anywhere = pl.BlockSpec(memory_space=pl.ANY)
    return pl.pallas_call(
        partial(head_kernel, n_head, n_z),
        out_shape=(out,) * 4,
        in_specs=[pl.BlockSpec(memory_space=pltpu.SMEM)] + [anywhere] * 4,
        out_specs=(anywhere,) * 4,
        scratch_shapes=[
            pltpu.VMEM((rows,) + tile, low),
            pltpu.VMEM((2 * rows,) + tile, low),
            pltpu.VMEM((2 * rows,) + tile, low),
            pltpu.VMEM((rows,) + tile, low),
            pltpu.VMEM((2 * rows,) + tile, wide),
            pltpu.VMEM((2 * rows,) + tile, wide),
            pltpu.VMEM((rows * PICKS + 1,) + tile, low),
            pltpu.VMEM((rows * PICKS + 1,) + tile, low),
        ]
        + [pltpu.VMEM((rows,) + tile, low)] * 8
        + [
            dma((4, rows)),
            dma((4, rows)),
            dma((2, rows)),
            dma((2, rows)),
            dma((4,)),
            dma((4, rows)),
            dma((4, rows)),
            dma((4, n_head)),
            dma((2,)),
            dma((2,)),
        ],
        compiler_params=pltpu.CompilerParams(
            collective_id=0, has_side_effects=True, vmem_limit_bytes=48 * 1024 * 1024
        ),
    )(stride_owner, queries, keys, values, grad_out)


def on_device(queries, keys, values, grad_out, stride_owner):
    n_head, n_blk = lax.axis_size("head"), lax.axis_size("blk")
    rows, width = queries.shape
    if rows == BLOCK and n_blk % 2 == 0 and width == n_head * (n_blk // 2) * HEAD_DIM:
        return by_heads(queries, keys, values, grad_out, stride_owner)
    return by_runs(queries, keys, values, grad_out, stride_owner)


def solution(mesh):
    return jax.shard_map(
        on_device,
        mesh=mesh,
        in_specs=(
            P(("blk", "head"), None),
            P(("blk", "head"), None),
            P(("blk", "head"), None),
            P(("blk", "head"), None),
            P(),
        ),
        out_specs=(P("blk", "head"), P("blk", "head"), P("blk", "head"), P("blk", "head")),
        check_vma=False,
    )
```

profile of v0, /device:TPU:9, one launch (start us, length us, event | category | flops | bytes accessed | tf_op | source)
XLA Modules:
  0.0 108.5 jit_solution(7455064220980836737)
XLA Ops:
  0.6 0.8 copy.9.owner_ref
  1.4 0.0 copy-start
  1.4 1.0 copy-done
  2.4 0.0 copy-start.1
  2.4 1.0 copy-done.1
  3.5 0.0 copy-start.2
  3.5 1.0 copy-done.2
  4.5 0.0 copy-start.3
  4.5 1.0 copy-done.3
  5.6 99.8 %shard_map.84 = (bf16[512,512]{1,0:T(8,128)(2,1)S(1)}, bf16[512,512]{1,0:T(8,128)(2,1)S(1)}, bf16[512,512]{1,0:T(8,128)(2,1)S(1)}, bf16[512,512]{1,0:T(8,128)(2,1)S(1)}) custom-call(s32[32,3]{1,0:T(8,128)S(1)} %copy.9.owner_ref, bf16[128,2048]{1,0:T(8,128)(2,1)S(1)} %copy-done, bf16[128,2048]{1,0:T(8,128)(2,1)S(1)} %copy-done.1, ...), custom_call_target="tpu_custom_call" | custom-call | tf_op jit(solution)/shard_map/pallas_call | solution.py:614
  105.4 0.8 copy.14
  106.2 0.8 copy.15
  107.0 0.8 copy.16
  107.8 0.8 copy.17
Async XLA Ops:
  1.4 1.0 copy-start
  2.4 1.0 copy-start.1
  3.5 1.0 copy-start.2
  4.5 1.0 copy-start.3
where the time goes:
time: 110 us; the launch traced here: 109 us
  Pallas kernels  99.8 us (91%)
  local copies, waits for them, and re-layouts  8.1 us (7%)
    pallas_call x1, Pallas kernels, by_heads(): pl.pallas_call(partial(head_kernel, n_head, n_z), out_shape=(out,) * 4, i...  99.8 us
    unnamed x13, local copies, waits for them, and re-layouts  8.1 us

commit v1 on v0

--- a/solution.py
+++ b/solution.py
@@ -274,7 +274,7 @@
 def head_kernel(
     n_head,
     n_z,
-    owner_ref,
+    owner_in,
     q_in,
     k_in,
     v_in,
@@ -283,6 +283,7 @@
     dq_out,
     dk_out,
     dv_out,
+    owner_ref,
     q_all,
     k_all,
     v_all,
@@ -367,7 +368,8 @@
         )
 
     sends = []
-    own_copies = []
+    own_copies = [pltpu.make_async_copy(owner_in, owner_ref, own_sem.at[4])]
+    own_copies[0].start()
     for at, source, target in key_pairs:
         own_copies.append(
             pltpu.make_async_copy(
@@ -466,7 +468,7 @@
         block = (2 * z1 + c) * runs + r
         low = (block + total_blocks - 1) % total_blocks
         high = (block + 1) % total_blocks
-        picks = [owner_ref[block, j] * runs + r for j in range(PICKS)]
+        picks = [owner_ref[j, block] * runs + r for j in range(PICKS)]
         named = [low, block, high] + picks + [0, 1]
         keys = jnp.concatenate([k_all[n] for n in named], axis=0)
         values = jnp.concatenate([v_all[n] for n in named], axis=0)
@@ -493,28 +495,25 @@
             v_far[row * PICKS + j] = value_terms[rows].astype(jnp.bfloat16)
 
     def hand_out(pairs, dz):
+        z2 = (z + n_z - dz) % n_z
         for at, stage, out in pairs:
-            z2 = (z + n_z - dz) % n_z
-            for r in range(runs):
-                source = stage.at[z2 * runs + r]
-                rows = pl.ds(r * BLOCK, BLOCK)
-                if dz == 0:
-                    copy = pltpu.make_async_copy(
-                        source, out.at[rows, columns(z)], out_own.at[at, r]
-                    )
-                    copy.start()
-                    own_outs.append(copy)
-                else:
-                    copy = pltpu.make_async_remote_copy(
-                        src_ref=source,
-                        dst_ref=out.at[rows, columns(z)],
-                        send_sem=out_send.at[at, z2 * runs + r],
-                        recv_sem=out_recv.at[at, z * runs + r],
-                        device_id={"head": head, "blk": 2 * z2 + c},
-                        device_id_type=MESH,
-                    )
-                    copy.start()
-                    sends.append(copy)
+            source = stage.at[pl.ds(z2 * runs, runs)]
+            target = out.at[:, :, columns(z)]
+            if dz == 0:
+                copy = pltpu.make_async_copy(source, target, out_own.at[at])
+                copy.start()
+                own_outs.append(copy)
+            else:
+                copy = pltpu.make_async_remote_copy(
+                    src_ref=source,
+                    dst_ref=target,
+                    send_sem=out_send.at[at, z2],
+                    recv_sem=out_recv.at[at, z],
+                    device_id={"head": head, "blk": 2 * z2 + c},
+                    device_id_type=MESH,
+                )
+                copy.start()
+                sends.append(copy)
 
     own_outs = []
     row_outs = ((0, o_stage, o_out), (1, dq_stage, dq_out))
@@ -542,7 +541,7 @@
             row = z1 * runs + r
             place = none
             for j in range(PICKS):
-                place = jnp.where(owner_ref[block, j] == run, row * PICKS + j, place)
+                place = jnp.where(owner_ref[j, block] == run, row * PICKS + j, place)
             total = total + far[place].astype(jnp.float32)
         return total
 
@@ -586,19 +585,43 @@
     for dz in range(1, n_z):
         z1 = (z + n_z - dz) % n_z
         for at, stage, out in row_outs + key_outs:
-            for r in range(runs):
-                pltpu.make_async_remote_copy(
-                    src_ref=stage.at[z1 * runs + r],
-                    dst_ref=out.at[pl.ds(r * BLOCK, BLOCK), columns(z1)],
-                    send_sem=out_send.at[at, z1 * runs + r],
-                    recv_sem=out_recv.at[at, z1 * runs + r],
-                    device_id=sibling,
-                    device_id_type=MESH,
-                ).wait_recv()
+            pltpu.make_async_remote_copy(
+                src_ref=stage.at[pl.ds(z1 * runs, runs)],
+                dst_ref=out.at[:, :, columns(z1)],
+                send_sem=out_send.at[at, z1],
+                recv_sem=out_recv.at[at, z1],
+                device_id=sibling,
+                device_id_type=MESH,
+            ).wait_recv()
     for copy in own_outs:
         copy.wait()
     for copy in sends + passes + pair_copies:
         copy.wait_send()
+
+
+def settle_kernel(count, pieces, *refs):
+    sources, targets = refs[:count], refs[count : 2 * count]
+    held, in_sem, out_sem = refs[2 * count :]
+    loads, stores = [], []
+    for at in range(count):
+        for piece in range(pieces):
+            loads.append(
+                pltpu.make_async_copy(
+                    sources[at].at[piece], held.at[at, piece], in_sem.at[at, piece]
+                )
+            )
+            stores.append(
+                pltpu.make_async_copy(
+                    held.at[at, piece], targets[at].at[piece], out_sem.at[at, piece]
+                )
+            )
+    for load in loads:
+        load.start()
+    for load, store in zip(loads, stores):
+        load.wait()
+        store.start()
+    for store in stores:
+        store.wait()
 
 
 def by_heads(queries, keys, values, grad_out, stride_owner):
@@ -609,14 +632,15 @@
     tile = (BLOCK, HEAD_DIM)
     low, wide = jnp.bfloat16, jnp.float32
     dma = pltpu.SemaphoreType.DMA
-    out = jax.ShapeDtypeStruct((seq_rows, width), low)
+    out = jax.ShapeDtypeStruct((n_head, BLOCK, width), low)
     anywhere = pl.BlockSpec(memory_space=pl.ANY)
-    return pl.pallas_call(
+    arrived = pl.pallas_call(
         partial(head_kernel, n_head, n_z),
         out_shape=(out,) * 4,
-        in_specs=[pl.BlockSpec(memory_space=pltpu.SMEM)] + [anywhere] * 4,
+        in_specs=[pl.BlockSpec(memory_space=pltpu.HBM)] * 5,
         out_specs=(anywhere,) * 4,
         scratch_shapes=[
+            pltpu.SMEM(stride_owner.shape[::-1], jnp.int32),
             pltpu.VMEM((rows,) + tile, low),
             pltpu.VMEM((2 * rows,) + tile, low),
             pltpu.VMEM((2 * rows,) + tile, low),
@@ -632,17 +656,30 @@
             dma((4, rows)),
             dma((2, rows)),
             dma((2, rows)),
+            dma((5,)),
+            dma((4, n_z)),
+            dma((4, n_z)),
             dma((4,)),
-            dma((4, rows)),
-            dma((4, rows)),
-            dma((4, n_head)),
             dma((2,)),
             dma((2,)),
         ],
         compiler_params=pltpu.CompilerParams(
-            collective_id=0, has_side_effects=True, vmem_limit_bytes=48 * 1024 * 1024
+            collective_id=0, has_side_effects=True, vmem_limit_bytes=67043328
         ),
-    )(stride_owner, queries, keys, values, grad_out)
+    )(stride_owner.T, queries, keys, values, grad_out)
+    settled = pl.pallas_call(
+        partial(settle_kernel, 4, n_head),
+        out_shape=(out,) * 4,
+        in_specs=[pl.BlockSpec(memory_space=pl.ANY)] * 4,
+        out_specs=(pl.BlockSpec(memory_space=pl.ANY),) * 4,
+        scratch_shapes=[
+            pltpu.VMEM((4, n_head, BLOCK, width), low),
+            dma((4, n_head)),
+            dma((4, n_head)),
+        ],
+        compiler_params=pltpu.CompilerParams(vmem_limit_bytes=67043328),
+    )(*arrived)
+    return tuple(part.reshape(seq_rows, width) for part in settled)
 
 
 def on_device(queries, keys, values, grad_out, stride_owner):

time: 110 us -> 103 us (0.936)
  local copies, waits for them, and re-layouts: 8.1 us -> 0 us
  Pallas kernels: 99.8 us -> 101 us
    unnamed x13 -> x0, local copies, waits for them, and re-layouts: 8.1 us -> none
    pallas_call x0 -> x1, Pallas kernels: none -> 2.57 us  [by_heads(): pl.pallas_call(partial(settle_kernel, 4, n_head), out_shape=(out,) * 4, i...]
    pallas_call x1, Pallas kernels: 99.8 us -> 98.3 us  [by_heads(): pl.pallas_call(partial(head_kernel, n_head, n_z), out_shape=(out,) * 4, i...]
where the time goes in v1:
time: 103 us; the launch traced here: 101 us
  Pallas kernels  101 us (98%)
    pallas_call x1, Pallas kernels, by_heads(): pl.pallas_call(partial(head_kernel, n_head, n_z), out_shape=(out,) * 4, i...  98.3 us
    pallas_call x1, Pallas kernels, by_heads(): pl.pallas_call(partial(settle_kernel, 4, n_head), out_shape=(out,) * 4, i...  2.57 us

profile of v1, /device:TPU:9, one launch (start us, length us, event | category | flops | bytes accessed | tf_op | source)
XLA Modules:
  0.0 101.5 jit_solution(8958950840557359974)
XLA Ops:
  0.6 98.3 %shard_map.84 = (bf16[4,128,512]{2,1,0:T(8,128)(2,1)}, bf16[4,128,512]{2,1,0:T(8,128)(2,1)}, bf16[4,128,512]{2,1,0:T(8,128)(2,1)}, bf16[4,128,512]{2,1,0:T(8,128)(2,1)}) custom-call(s32[3,32]{1,0:T(4,128)} %bitcast.5, bf16[128,2048]{1,0:T(8,128)(2,1)} %q_in.1, bf16[128,2048]{1,0:T(8,128)(2,1)} %k_in.1, bf16[128,2048]{1,0:T(8,128)(2,1)} %v_in.1, ...), custom_call_target="tpu_custom_call" | custom-call | tf_op jit(solution)/shard_map/pallas_call | solution.py:637
  98.9 2.6 %shard_map.85 = (bf16[4,128,512]{2,1,0:T(8,128)(2,1)}, bf16[4,128,512]{2,1,0:T(8,128)(2,1)}, bf16[4,128,512]{2,1,0:T(8,128)(2,1)}, bf16[4,128,512]{2,1,0:T(8,128)(2,1)}) custom-call(bf16[4,128,512]{2,1,0:T(8,128)(2,1)} %get-tuple-element.12.refs_0_, bf16[4,128,512]{2,1,0:T(8,128)(2,1)} %get-tuple-element.13.refs_1_, ...), custom_call_target="tpu_custom_call" | custom-call | tf_op jit(solution)/shard_map/pallas_call | solution.py:670

commit v2 on v1

--- a/solution.py
+++ b/solution.py
@@ -321,7 +321,7 @@
     sibling = {"head": head, "blk": 2 * z + 1 - c}
     offsets = [(dz, dh) for dz in range(n_z) for dh in range(n_head)]
     far_first = [dz for dz in (2, 1, 3, 0) if dz < n_z] + list(range(4, n_z))
-    near_first = [0] + [dz for dz in far_first if dz != 0][::-1]
+    near_first = far_first
 
     def columns(head_id):
         return pl.ds(pl.multiple_of(head_id * HEAD_DIM, HEAD_DIM), HEAD_DIM)
@@ -619,7 +619,7 @@
         load.start()
     for load, store in zip(loads, stores):
         load.wait()
-        store.start()
+        store.start(priority=1)
     for store in stores:
         store.wait()
 

time: 103 us -> 102 us (level); the launches traced: 101 us -> 102 us
  no operation moved by 1% of the time
where the time goes in v2:
time: 102 us
  Pallas kernels  101 us (99%)
    pallas_call x1, Pallas kernels, by_heads(): pl.pallas_call(partial(head_kernel, n_head, n_z), out_shape=(out,) * 4, i...  98.5 us
    pallas_call x1, Pallas kernels, by_heads(): pl.pallas_call(partial(settle_kernel, 4, n_head), out_shape=(out,) * 4, i...  2.57 us

profile of v2, /device:TPU:9, one launch (start us, length us, event | category | flops | bytes accessed | tf_op | source)
XLA Modules:
  0.0 101.7 jit_solution(18050954632401376619)
XLA Ops:
  0.6 98.5 %shard_map.84 = (bf16[4,128,512]{2,1,0:T(8,128)(2,1)}, bf16[4,128,512]{2,1,0:T(8,128)(2,1)}, bf16[4,128,512]{2,1,0:T(8,128)(2,1)}, bf16[4,128,512]{2,1,0:T(8,128)(2,1)}) custom-call(s32[3,32]{1,0:T(4,128)} %bitcast.5, bf16[128,2048]{1,0:T(8,128)(2,1)} %q_in.1, bf16[128,2048]{1,0:T(8,128)(2,1)} %k_in.1, bf16[128,2048]{1,0:T(8,128)(2,1)} %v_in.1, ...), custom_call_target="tpu_custom_call" | custom-call | tf_op jit(solution)/shard_map/pallas_call | solution.py:637
  99.1 2.6 %shard_map.85 = (bf16[4,128,512]{2,1,0:T(8,128)(2,1)}, bf16[4,128,512]{2,1,0:T(8,128)(2,1)}, bf16[4,128,512]{2,1,0:T(8,128)(2,1)}, bf16[4,128,512]{2,1,0:T(8,128)(2,1)}) custom-call(bf16[4,128,512]{2,1,0:T(8,128)(2,1)} %get-tuple-element.12.refs_0_, bf16[4,128,512]{2,1,0:T(8,128)(2,1)} %get-tuple-element.13.refs_1_, ...), custom_call_target="tpu_custom_call" | custom-call | tf_op jit(solution)/shard_map/pallas_call | solution.py:670
